TPU v7x, 32 devices: a whole 2x2x4 slice. The times are simulated.
32 devices in a mesh: groups: 2 (over y), seq: 4 (over z), fsdp: 4 (over x, core).
Axes of the slice: x: 2, y: 2, z: 4, core: 2. Of those that a mesh axis runs over, the one named last changes fastest.
Arguments:
- tokens: bfloat16 [1024, 1024], P(('groups', 'seq')), parts along dimension 0, may hold values from -16 to 16
- qkv_weight: bfloat16 [1024, 1536], P('seq', 'fsdp'), may hold values from -0.125 to 0.125
- covisible: int32 [8, 4], P('groups'), parts along dimension 0, may hold values 0 or 1
- block_drive: int32 [8], P('groups'), parts along dimension 0, may hold values from 0 to 2
- grad_out: bfloat16 [1024, 512], P(('groups', 'seq'), 'fsdp'), parts along dimension 0, may hold values from -6 to 6
Outputs:
- attention: bfloat16 [1024, 512], P(('groups', 'seq'), 'fsdp'), parts along dimension 0
- grad_input: bfloat16 [1024, 1024], P(('groups', 'seq'), 'fsdp'), parts along dimension 0
- grad_weight: float32 [2048, 1536], P(('groups', 'seq'), 'fsdp'), parts along dimension 0
There are 2 independent parts, one for each index of `groups`. A program takes and returns all parts, laid end to end along the dimension named above; an argument that names none is the same for every part. Nothing has to cross between parts.
All inputs are finite; a program needn't handle non-finite values.
Results may differ from a plain program's by a relative error of at most 0.018.
The roundings to bfloat16 on the way count: a program that leaves them out, or rounds other values in their place, can miss the bound.
Values may be sent and summed in bfloat16 or wider, within the bound.
No kernel may reach another device: no remote copies, remote signals or barrier semaphores. Data moves between devices by JAX's collectives and lax.ppermute only.
A program may use at most 64 MiB of HBM per device.

v0:
```python
import jax
import jax.numpy as jnp
from jax import lax
from jax.sharding import PartitionSpec as P

HD = 64
BLOCK = 128
MASKED_SCORE = -1e30


def query_visible(covisible, block_drive, first_block, block_count):
    own_rows = lax.dynamic_slice_in_dim(covisible, first_block, block_count, 0)
    own_drive = lax.dynamic_slice_in_dim(block_drive, first_block, block_count, 0)
    joined = jnp.logical_or(own_rows == 1, own_drive[:, None] == block_drive[None, :])
    return joined.astype(jnp.float32)


def key_visible(covisible, block_drive, first_block, block_count):
    own_columns = lax.dynamic_slice_in_dim(covisible, first_block, block_count, 1)
    own_drive = lax.dynamic_slice_in_dim(block_drive, first_block, block_count, 0)
    joined = jnp.logical_or(own_columns == 1, block_drive[:, None] == own_drive[None, :])
    return joined.astype(jnp.float32)


def block_onehot(length, block_total):
    member = lax.iota(jnp.int32, length) // BLOCK
    return (member[:, None] == lax.iota(jnp.int32, block_total)[None, :]).astype(jnp.float32)


def per_device(tokens, qkv_weight, covisible, block_drive, grad_out):
    local_rows = tokens.shape[0]
    seq_count = lax.axis_size("seq")
    seq_index = lax.axis_index("seq")
    out_width = qkv_weight.shape[1]
    local_heads = out_width // (3 * HD)
    block_count = local_rows // BLOCK
    block_total = covisible.shape[0]
    first_block = seq_index * block_count
    scaling = HD ** (-0.5)
    rows_visible = query_visible(covisible, block_drive, first_block, block_count)
    columns_visible = key_visible(covisible, block_drive, first_block, block_count)
    inputs = tokens
    projected = jnp.dot(
        inputs,
        lax.all_gather(qkv_weight, "seq", axis=0, tiled=True),
        preferred_element_type=jnp.float32,
    )
    projected = projected.astype(jnp.bfloat16).reshape(local_rows, local_heads, 3, HD)
    queries = projected[:, :, 0, :]
    local_keys = projected[:, :, 1, :]
    local_values = projected[:, :, 2, :]
    key_value = projected[:, :, 1:, :].reshape(local_rows, local_heads * 2 * HD)

    def local_visible(length):
        onehot = block_onehot(length, block_total)
        return (jnp.repeat(jnp.dot(rows_visible, onehot.T), BLOCK, axis=0) > 0.5)[None]

    panel = lax.all_gather(key_value, "seq", axis=0, tiled=True)
    running_max = jnp.full((local_heads, local_rows), MASKED_SCORE, jnp.float32)
    length = panel.shape[0]
    visible = local_visible(length)
    split_panel = panel.reshape(length, local_heads, 2, HD)
    scores = (
        jnp.einsum(
            "qhd,khd->hqk", queries, split_panel[:, :, 0, :], preferred_element_type=jnp.float32
        )
        * scaling
    )
    new_max = jnp.maximum(running_max, jnp.where(visible, scores, MASKED_SCORE).max(axis=2))
    shifted = jnp.exp(jnp.where(visible, scores - new_max[:, :, None], MASKED_SCORE))
    running_sum = shifted.sum(axis=2)
    wide_values = split_panel[:, :, 1, :].astype(jnp.float32)
    weighted = jnp.einsum(
        "hqk,khd->hqd",
        shifted,
        wide_values,
        precision=lax.Precision.HIGHEST,
        preferred_element_type=jnp.float32,
    )
    running_max, running_sum, weighted = (new_max, running_sum, weighted)
    attention_heads = (weighted / running_sum[:, :, None]).astype(jnp.bfloat16)
    attention = jnp.transpose(attention_heads, (1, 0, 2)).reshape(local_rows, local_heads * HD)
    log_total = running_max + jnp.log(running_sum)
    grad_heads = grad_out.reshape(local_rows, local_heads, HD)
    grad_dot_rows = jnp.sum(
        grad_heads.astype(jnp.float32)
        * attention.reshape(local_rows, local_heads, HD).astype(jnp.float32),
        axis=2,
    )
    grad_dot = jnp.transpose(grad_dot_rows)
    log_total_rows = jnp.transpose(log_total)
    all_log_total, all_grad_dot = (
        lax.all_gather(log_total_rows, "seq", axis=0, tiled=True),
        lax.all_gather(grad_dot_rows, "seq", axis=0, tiled=True),
    )
    query_rows = queries.reshape(local_rows, local_heads * HD)
    far_queries = lax.all_gather(query_rows, "seq", axis=0, tiled=True)
    far_grads = lax.all_gather(grad_out, "seq", axis=0, tiled=True)
    length = far_queries.shape[0]
    onehot = block_onehot(length, block_total)
    visible = (jnp.repeat(jnp.dot(onehot, columns_visible), BLOCK, axis=1) > 0.5)[None]
    far_heads = far_queries.reshape(length, local_heads, HD)
    far_grad_heads = far_grads.reshape(length, local_heads, HD)
    far_log_total = jnp.transpose(all_log_total)
    far_grad_dot = jnp.transpose(all_grad_dot)
    scores = (
        jnp.einsum("qhd,khd->hqk", far_heads, local_keys, preferred_element_type=jnp.float32)
        * scaling
    )
    probabilities = jnp.exp(jnp.where(visible, scores - far_log_total[:, :, None], MASKED_SCORE))
    grad_prob = jnp.einsum(
        "qhd,khd->hqk", far_grad_heads, local_values, preferred_element_type=jnp.float32
    )
    grad_score = (probabilities * (grad_prob - far_grad_dot[:, :, None]) * scaling).astype(
        jnp.bfloat16
    )
    grad_keys = jnp.einsum(
        "hqk,qhd->khd", grad_score, far_heads, preferred_element_type=jnp.float32
    )
    grad_values = jnp.einsum(
        "hqk,qhd->khd",
        probabilities.astype(jnp.bfloat16),
        far_grad_heads,
        preferred_element_type=jnp.float32,
    )
    grad_keys, grad_values = (grad_keys, grad_values)
    panel = lax.all_gather(key_value, "seq", axis=0, tiled=True)
    length = panel.shape[0]
    visible = local_visible(length)
    split_panel = panel.reshape(length, local_heads, 2, HD)
    panel_keys = split_panel[:, :, 0, :]
    scores = (
        jnp.einsum("qhd,khd->hqk", queries, panel_keys, preferred_element_type=jnp.float32)
        * scaling
    )
    probabilities = jnp.exp(jnp.where(visible, scores - log_total[:, :, None], MASKED_SCORE))
    grad_prob = jnp.einsum(
        "qhd,khd->hqk", grad_heads, split_panel[:, :, 1, :], preferred_element_type=jnp.float32
    )
    grad_score = (probabilities * (grad_prob - grad_dot[:, :, None]) * scaling).astype(jnp.bfloat16)
    grad_queries = jnp.einsum(
        "hqk,khd->qhd", grad_score, panel_keys, preferred_element_type=jnp.float32
    )
    grad_qkv = (
        jnp.stack([grad_queries, grad_keys, grad_values], axis=2)
        .astype(jnp.bfloat16)
        .reshape(local_rows, out_width)
    )
    partial_input = lax.dot_general(
        grad_qkv,
        lax.all_gather(qkv_weight, "seq", axis=0, tiled=True),
        (((1,), (1,)), ((), ())),
        preferred_element_type=jnp.float32,
    )
    grad_input = lax.psum_scatter(partial_input, "fsdp", scatter_dimension=1, tiled=True).astype(
        jnp.bfloat16
    )
    token_scale = (local_rows * seq_count) ** (-0.5)
    column_tokens = lax.all_to_all(tokens, "seq", split_axis=1, concat_axis=0, tiled=True)
    inputs = column_tokens
    summed_rows = lax.dot_general(
        inputs,
        lax.all_gather(grad_qkv, "seq", axis=0, tiled=True),
        (((0,), (0,)), ((), ())),
        preferred_element_type=jnp.float32,
    )
    grad_weight = summed_rows * token_scale
    return (attention, grad_input, grad_weight)


def solution(mesh):
    in_specs = (
        P(("groups", "seq"), None),
        P("seq", "fsdp"),
        P("groups", None),
        P("groups"),
        P(("groups", "seq"), "fsdp"),
    )
    out_specs = (
        P(("groups", "seq"), "fsdp"),
        P(("groups", "seq"), "fsdp"),
        P(("groups", "seq"), "fsdp"),
    )
    return jax.shard_map(
        per_device, mesh=mesh, in_specs=in_specs, out_specs=out_specs, check_vma=False
    )
```

profile of v0, /device:TPU:0, one launch (start us, length us, event | category | flops | bytes accessed | tf_op | source)
XLA Modules:
  0.0 121.6 jit_solution(15169649852441177908)
XLA Ops:
  7.2 0.6 copy-done.3
  7.9 0.6 dynamic_slice.11
  8.6 0.9 fusion.35
  9.5 21.6 %all_gather.23 = bf16[1024,384]{1,0:T(8,128)(2,1)S(1)} all-gather(bf16[256,384]{1,0:T(8,128)(2,1)} %param.6), channel_id=1, replica_groups=mesh['groups'=2,'seq'=4,'fsdp'=4] {'seq'}, dimensions={0}, use_global_device_ids=true | all-gather | bytes 983040 | tf_op jit(solution)/shard_map/all_gather | solution.py:45
  31.1 0.3 convolution_convert_fusion
  31.4 0.1 copy.26
  31.6 12.8 %all_gather.24 = bf16[512,256]{0,1:T(8,128)(2,1)S(1)} all-gather(bf16[128,256]{0,1:T(8,128)(2,1)S(1)} %bitcast.145), channel_id=1, replica_groups=mesh['groups'=2,'seq'=4,'fsdp'=4] {'seq'}, dimensions={0}, use_global_device_ids=true | all-gather | bytes 327680 | tf_op jit(solution)/shard_map/all_gather | solution.py:58
  44.4 0.3 select_reduce_fusion
  44.7 0.2 fusion.24
  45.1 0.8 copy-done.1
  45.8 0.1 copy.30
  45.9 13.3 %all_gather.27 = bf16[512,128]{1,0:T(8,128)(2,1)S(1)} all-gather(bf16[128,128]{1,0:T(8,128)(2,1)S(1)} %copy-done.1), channel_id=1, replica_groups=mesh['groups'=2,'seq'=4,'fsdp'=4] {'seq'}, dimensions={0}, use_global_device_ids=true | all-gather | bytes 163840 | tf_op jit(solution)/shard_map/all_gather | solution.py:98
  59.3 8.2 %all_gather.26 = f32[512,2]{0,1:T(2,128)S(1)} all-gather(f32[128,2]{0,1:T(2,128)S(1)} %bitcast_add_fusion), channel_id=1, replica_groups=mesh['groups'=2,'seq'=4,'fsdp'=4] {'seq'}, dimensions={0}, use_global_device_ids=true | all-gather | bytes 5120 | tf_op jit(solution)/shard_map/all_gather | solution.py:93
  67.6 0.9 fusion.34
  68.5 12.3 %all_gather.25 = bf16[512,128]{0,1:T(8,128)(2,1)S(1)} all-gather(bf16[128,128]{0,1:T(8,128)(2,1)S(1)} %bitcast.146), channel_id=1, replica_groups=mesh['groups'=2,'seq'=4,'fsdp'=4] {'seq'}, dimensions={0}, use_global_device_ids=true | all-gather | bytes 163840 | tf_op jit(solution)/shard_map/all_gather | solution.py:97
  80.8 0.6 multiply_reduce_fusion
  81.3 8.0 %all_gather.28 = f32[512,2]{0,1:T(2,128)S(1)} all-gather(f32[128,2]{0,1:T(2,128)S(1)} %get-tuple-element.14), channel_id=1, replica_groups=mesh['groups'=2,'seq'=4,'fsdp'=4] {'seq'}, dimensions={0}, use_global_device_ids=true | all-gather | bytes 5120 | tf_op jit(solution)/shard_map/all_gather | solution.py:94
  89.4 0.1 copy.34
  89.5 0.4 fusion.6
  89.9 0.2 fusion.20
  90.1 0.4 fusion.19
  90.5 0.5 fusion.18
  91.0 1.2 fusion.62
  92.2 0.8 copy.37
  93.0 3.4 %all-to-all-start = ((bf16[128,4,256]{0,2,1:T(8,128)(2,1)}), bf16[128,4,256]{0,2,1:T(8,128)(2,1)S(1)}, u32[]{:S(2)}, u32[]{:S(2)}) async-start(bf16[128,4,256]{0,2,1:T(8,128)(2,1)} %bitcast.36), calls=%async_computation.1 | async-start | bytes 524288 | tf_op jit(solution)/shard_map/all_to_all | solution.py:159
  96.5 0.7 copy.39
  97.2 14.2 %all_gather.29 = bf16[512,384]{0,1:T(8,128)(2,1)S(1)} all-gather(bf16[128,384]{0,1:T(8,128)(2,1)S(1)} %bitcast.134), channel_id=1, replica_groups=mesh['groups'=2,'seq'=4,'fsdp'=4] {'seq'}, dimensions={0}, use_global_device_ids=true | all-gather | bytes 491520 | tf_op jit(solution)/shard_map/all_gather | solution.py:163
  111.4 0.1 copy.38
  111.6 0.3 fusion.11
  111.8 0.9 copy.40
  112.7 0.5 reduce-scatter.2.cloned.1.call-done
  113.2 1.5 %convert_element_type.44 = bf16[128,256]{1,0:T(8,128)(2,1)} convert(f32[128,256]{1,0:T(8,128)} %reduce-scatter.2.cloned.1.call-done) | non-fusion elementwise | flops 32768 | bytes 196608 | tf_op jit(solution)/shard_map/convert_element_type | solution.py:155
  (21 shorter events, 0.4 us)
Async XLA Ops:
  7.2 106.1 %reduce-scatter.2.cloned.1.call-start = ((), (), s32[]{:S(2)}) async-start(), calls=%async_computation.2 | async-start | bytes 655360 | tf_op jit(solution)/shard_map/reduce_scatter | solution.py:155
  7.2 0.7 copy-start.3
  7.9 0.7 copy-start.2
  9.5 21.6 %copy-start = (bf16[128,1024]{1,0:T(8,128)(2,1)S(1)}, bf16[128,1024]{1,0:T(8,128)(2,1)}, u32[]{:S(2)}) copy-start(bf16[128,1024]{1,0:T(8,128)(2,1)} %param.5) | copy-start | bytes 786436
  45.1 0.8 copy-start.1
  93.0 18.4 %all-to-all-start = ((bf16[128,4,256]{0,2,1:T(8,128)(2,1)}), bf16[128,4,256]{0,2,1:T(8,128)(2,1)S(1)}, u32[]{:S(2)}, u32[]{:S(2)}) async-start(bf16[128,4,256]{0,2,1:T(8,128)(2,1)} %bitcast.36), calls=%async_computation.1 | async-start | bytes 524288 | tf_op jit(solution)/shard_map/all_to_all | solution.py:159
Sparse Core Ops, SparseCore 0:
  92.3 20.8 reduce-scatter.1
where the time goes:
time: 122 us
  blocking collectives  90.5 us (74%)
  between operations  14.2 us (12%)
  matrix products  5.87 us (5%)
  local copies, waits for them, and re-layouts  5.24 us (4%)
  starting transfers between devices  3.44 us (3%)
  other arithmetic  1.84 us (2%)
    all_gather x1, blocking collectives, per_device(): lax.all_gather(qkv_weight, 'seq', axis=0, tiled=True)  21.6 us
    all_gather x1, blocking collectives, per_device(): lax.all_gather(grad_qkv, 'seq', axis=0, tiled=True)  14.2 us
    all_gather x1, blocking collectives, per_device(): far_grads = lax.all_gather(grad_out, 'seq', axis=0, tiled=True)  13.3 us
    all_gather x1, blocking collectives, per_device(): panel = lax.all_gather(key_value, 'seq', axis=0, tiled=True)  12.8 us
    all_gather x1, blocking collectives, per_device(): far_queries = lax.all_gather(query_rows, 'seq', axis=0, tiled=True)  12.3 us
    all_gather x1, blocking collectives, per_device(): lax.all_gather(log_total_rows, 'seq', axis=0, tiled=True)  8.22 us
    all_gather x1, blocking collectives, per_device(): lax.all_gather(grad_dot_rows, 'seq', axis=0, tiled=True)  8.03 us
    unnamed x13, local copies, waits for them, and re-layouts  4.19 us
  transfers between devices with their start and end apart: 2, of which 1 were waited for; matrix products, arithmetic and copies ran while one was open for 2% of the time, Pallas kernels for 0%

commit v1 on v0

--- a/solution.py
+++ b/solution.py
@@ -94,8 +94,11 @@
         lax.all_gather(grad_dot_rows, "seq", axis=0, tiled=True),
     )
     query_rows = queries.reshape(local_rows, local_heads * HD)
-    far_queries = lax.all_gather(query_rows, "seq", axis=0, tiled=True)
-    far_grads = lax.all_gather(grad_out, "seq", axis=0, tiled=True)
+    far_queries, far_grads = jnp.split(
+        lax.all_gather(jnp.concatenate([query_rows, grad_out], axis=1), "seq", axis=0, tiled=True),
+        [query_rows.shape[1]],
+        axis=1,
+    )
     length = far_queries.shape[0]
     onehot = block_onehot(length, block_total)
     visible = (jnp.repeat(jnp.dot(onehot, columns_visible), BLOCK, axis=1) > 0.5)[None]

time: 122 us -> 111 us (0.910)
  blocking collectives: 90.5 us -> 79.7 us
    all_gather x2 -> x1, blocking collectives: 25.6 us -> 13.8 us  [per_device(): lax.all_gather(jnp.concatenate([query_rows, grad_out], axis=1), 'seq', ax...]
  transfers between devices with their start and end apart: 2 -> 2, of which waited for: 1 -> 0; matrix products, arithmetic and copies ran while one was open for 2% -> 3% of each run, Pallas kernels for 0% -> 0%
where the time goes in v1:
time: 111 us
  blocking collectives  79.7 us (72%)
  between operations  14.2 us (13%)
  matrix products  5.87 us (5%)
  local copies, waits for them, and re-layouts  5.49 us (5%)
  starting transfers between devices  3.45 us (3%)
  other arithmetic  1.85 us (2%)
    all_gather x1, blocking collectives, per_device(): lax.all_gather(qkv_weight, 'seq', axis=0, tiled=True)  21.6 us
    all_gather x1, blocking collectives, per_device(): lax.all_gather(grad_qkv, 'seq', axis=0, tiled=True)  14.2 us
    all_gather x1, blocking collectives, per_device(): lax.all_gather(jnp.concatenate([query_rows, grad_out], axis=1), 'seq', ax...  13.8 us
    all_gather x1, blocking collectives, per_device(): panel = lax.all_gather(key_value, 'seq', axis=0, tiled=True)  12.8 us
    all_gather x1, blocking collectives, per_device(): lax.all_gather(grad_dot_rows, 'seq', axis=0, tiled=True)  9.21 us
    all_gather x1, blocking collectives, per_device(): lax.all_gather(log_total_rows, 'seq', axis=0, tiled=True)  8.07 us
    unnamed x13, local copies, waits for them, and re-layouts  4.19 us
    all_to_all x1, starting transfers between devices, per_device(): lax.all_to_all(tokens, 'seq', split_axis=1, concat_axis=0, tiled=True)  3.41 us
  transfers between devices with their start and end apart: 2, of which 0 were waited for; matrix products, arithmetic and copies ran while one was open for 3% of the time, Pallas kernels for 0%

profile of v1, /device:TPU:0, one launch (start us, length us, event | category | flops | bytes accessed | tf_op | source)
XLA Modules:
  0.0 110.6 jit_solution(4485363590695219461)
XLA Ops:
  7.2 0.6 copy-done.3
  7.9 0.6 dynamic_slice.11
  8.6 0.9 fusion.34
  9.5 21.6 %all_gather.20 = bf16[1024,384]{1,0:T(8,128)(2,1)S(1)} all-gather(bf16[256,384]{1,0:T(8,128)(2,1)} %param.6), channel_id=1, replica_groups=mesh['groups'=2,'seq'=4,'fsdp'=4] {'seq'}, dimensions={0}, use_global_device_ids=true | all-gather | bytes 983040 | tf_op jit(solution)/shard_map/all_gather | solution.py:45
  31.1 0.3 convolution_convert_fusion
  31.4 0.1 copy.30
  31.6 12.8 %all_gather.21 = bf16[512,256]{0,1:T(8,128)(2,1)S(1)} all-gather(bf16[128,256]{0,1:T(8,128)(2,1)S(1)} %bitcast.131), channel_id=1, replica_groups=mesh['groups'=2,'seq'=4,'fsdp'=4] {'seq'}, dimensions={0}, use_global_device_ids=true | all-gather | bytes 327680 | tf_op jit(solution)/shard_map/all_gather | solution.py:58
  44.3 0.3 select_reduce_fusion
  44.7 0.2 fusion.23
  45.1 0.8 copy-done.1
  45.8 0.1 copy.34
  45.9 8.1 %all_gather.23 = f32[512,2]{0,1:T(2,128)S(1)} all-gather(f32[128,2]{0,1:T(2,128)S(1)} %bitcast_add_fusion), channel_id=1, replica_groups=mesh['groups'=2,'seq'=4,'fsdp'=4] {'seq'}, dimensions={0}, use_global_device_ids=true | all-gather | bytes 5120 | tf_op jit(solution)/shard_map/all_gather | solution.py:93
  54.1 0.9 fusion.33
  55.0 0.1 copy.36
  55.1 13.8 %all_gather.22 = bf16[512,256]{1,0:T(8,128)(2,1)S(1)} all-gather(bf16[128,256]{1,0:T(8,128)(2,1)S(1)} %pad_maximum_fusion.1), channel_id=1, replica_groups=mesh['groups'=2,'seq'=4,'fsdp'=4] {'seq'}, dimensions={0}, use_global_device_ids=true | all-gather | bytes 327680 | tf_op jit(solution)/shard_map/all_gather | solution.py:98
  69.0 0.1 copy.37
  69.1 0.6 multiply_reduce_fusion
  69.7 9.2 %all_gather.24 = f32[512,2]{0,1:T(2,128)S(1)} all-gather(f32[128,2]{0,1:T(2,128)S(1)} %get-tuple-element.16), channel_id=1, replica_groups=mesh['groups'=2,'seq'=4,'fsdp'=4] {'seq'}, dimensions={0}, use_global_device_ids=true | all-gather | bytes 5120 | tf_op jit(solution)/shard_map/all_gather | solution.py:94
  78.9 0.1 copy.40
  79.0 0.4 fusion.5
  79.4 0.2 fusion.19
  79.5 0.4 fusion.18
  80.0 0.5 fusion.17
  80.5 1.2 %fusion.62 = f32[128,1024]{1,0:T(8,128)} fusion(bf16[128,384]{0,1:T(8,128)(2,1)S(1)} %bitcast.119, bf16[1024,384]{1,0:T(8,128)(2,1)S(1)} %all_gather.20), kind=kOutput, calls=%fused_computation.92 | convolution fusion | flops 100663296 | bytes 1409024 | tf_op jit(solution)/shard_map/dot_general | solution.py:152
  81.7 0.8 copy.42
  82.5 3.4 %all-to-all-start = ((bf16[128,4,256]{0,2,1:T(8,128)(2,1)}), bf16[128,4,256]{0,2,1:T(8,128)(2,1)S(1)}, u32[]{:S(2)}, u32[]{:S(2)}) async-start(bf16[128,4,256]{0,2,1:T(8,128)(2,1)} %bitcast.35), calls=%async_computation.1 | async-start | bytes 524288 | tf_op jit(solution)/shard_map/all_to_all | solution.py:162
  85.9 0.7 copy.44
  86.7 14.2 %all_gather.25 = bf16[512,384]{0,1:T(8,128)(2,1)S(1)} all-gather(bf16[128,384]{0,1:T(8,128)(2,1)S(1)} %bitcast.120), channel_id=1, replica_groups=mesh['groups'=2,'seq'=4,'fsdp'=4] {'seq'}, dimensions={0}, use_global_device_ids=true | all-gather | bytes 491520 | tf_op jit(solution)/shard_map/all_gather | solution.py:166
  100.9 0.1 copy.43
  101.0 0.3 fusion.10
  101.3 0.9 copy.45
  102.2 1.5 %convert_element_type.44 = bf16[128,256]{1,0:T(8,128)(2,1)} convert(f32[128,256]{1,0:T(8,128)} %reduce-scatter.2.cloned.1.call-done) | non-fusion elementwise | flops 32768 | bytes 196608 | tf_op jit(solution)/shard_map/convert_element_type | solution.py:158
  (24 shorter events, 0.4 us)
Async XLA Ops:
  7.2 95.1 %reduce-scatter.2.cloned.1.call-start = ((), (), s32[]{:S(2)}) async-start(), calls=%async_computation.2 | async-start | bytes 655360 | tf_op jit(solution)/shard_map/reduce_scatter | solution.py:158
  7.2 0.7 copy-start.3
  7.9 0.7 copy-start.2
  9.5 21.6 %copy-start = (bf16[128,1024]{1,0:T(8,128)(2,1)S(1)}, bf16[128,1024]{1,0:T(8,128)(2,1)}, u32[]{:S(2)}) copy-start(bf16[128,1024]{1,0:T(8,128)(2,1)} %param.5) | copy-start | bytes 786436
  45.1 0.8 copy-start.1
  82.5 18.4 %all-to-all-start = ((bf16[128,4,256]{0,2,1:T(8,128)(2,1)}), bf16[128,4,256]{0,2,1:T(8,128)(2,1)S(1)}, u32[]{:S(2)}, u32[]{:S(2)}) async-start(bf16[128,4,256]{0,2,1:T(8,128)(2,1)} %bitcast.35), calls=%async_computation.1 | async-start | bytes 524288 | tf_op jit(solution)/shard_map/all_to_all | solution.py:162
Sparse Core Ops, SparseCore 0:
  81.8 19.8 reduce-scatter.1
